TPU v7x, 256 devices: a whole 4x4x8 slice. The times are simulated.
256 devices in a mesh: pts: 32 (over y, z), own: 8 (over x, core).
Axes of the slice: x: 4, y: 4, z: 8, core: 2. Of those that a mesh axis runs over, the one named last changes fastest.
Arguments:
- points: bfloat16 [65536, 1536], P(('pts', 'own')), may hold values from -6 to 6
- parent_of: int32 [65536, 1], P('pts'), may hold values from 0 to 127, as said below
- owner_of: int32 [128], replicated, may hold values from 0 to 7, as said below
- child_count: int32 [128], replicated, may hold values from 16 to 64, as said below
- centroids: bfloat16 [8, 1024, 1536], P('own'), may hold values from -6 to 6
Outputs:
- new_centroids: bfloat16 [8, 1024, 1536], P('own', 'pts')
Inputs may be any that keep to these rules, and one draw needn't show every extreme that they name: `owner_of`: each owner is named by exactly 16 parents. `child_count`: exactly 64 for at least one parent. `parent_of`: every parent is named by some point; in the 256 rows of one device, exactly 64 rows have parents of one owner, and all devices with the same pts index pick the same such owner; the rest of the device's rows go to the other owners as evenly as possible, so no owner gets more than 64 rows of one device.
All inputs are finite; a program needn't handle non-finite values.
Results may differ from a plain program's by a relative error of at most 0.0031.
Values may be sent and summed in bfloat16 or wider, within the bound.
A program may use at most 128 MiB of HBM per device.

v0:
```python
import jax
import jax.numpy as jnp
from jax import lax
from jax.sharding import PartitionSpec as P

SWEEPS = 2


def unit_rms(values):
    values = values.astype(jnp.float32)
    return values * lax.rsqrt(jnp.mean(values * values, axis=-1, keepdims=True) + 1e-06)


def lookup(onehot, table):
    return jnp.sum(jnp.where(onehot, table[None, :], 0), axis=1)


def local(points, parent_of, owner_of, child_count, centroids):
    width = points.shape[1]
    point_unit = unit_rms(points).astype(jnp.bfloat16)
    parent_ids = parent_of[:, 0]
    parent_range = jnp.arange(owner_of.shape[0], dtype=jnp.int32)
    same_owner = owner_of[:, None] == owner_of[None, :]
    earlier = parent_range[None, :] < parent_range[:, None]
    first_slot = jnp.sum(jnp.where(same_owner & earlier, child_count[None, :], 0), axis=1)
    owner_index = lax.axis_index("own")
    cent_unit = unit_rms(centroids[0]).astype(jnp.bfloat16)
    slot_total = cent_unit.shape[0]
    slot_index = jnp.arange(slot_total, dtype=jnp.int32)
    rows = lax.all_gather(point_unit, "own", axis=0, tiled=True)
    onehot = parent_ids[:, None] == parent_range[None, :]
    row_owner = lookup(onehot, owner_of)
    row_first = lookup(onehot, first_slot)
    row_count = lookup(onehot, child_count)
    row_live = row_owner == owner_index
    in_range = (
        row_live[:, None]
        & (slot_index[None, :] >= row_first[:, None])
        & (slot_index[None, :] < (row_first + row_count)[:, None])
    )
    table_range = (
        (owner_of == owner_index)[:, None]
        & (slot_index[None, :] >= first_slot[:, None])
        & (slot_index[None, :] < (first_slot + child_count)[:, None])
    )
    slot_used = jnp.any(table_range, axis=0)
    scores = jnp.dot(rows, cent_unit.T, preferred_element_type=jnp.float32) / (width * 0.05)
    weights = jnp.where(in_range, jnp.exp(scores), jnp.float32(0.0))
    for sweep in range(SWEEPS):
        column_sum = lax.psum(jnp.sum(weights, axis=0), "pts")
        weights = weights / jnp.where(slot_used, column_sum, jnp.float32(1.0))[None, :]
        row_sum = jnp.sum(weights, axis=1)
        weights = weights / jnp.where(row_live, row_sum, jnp.float32(1.0))[:, None]
    assign = weights.astype(jnp.bfloat16)
    share = slot_total // lax.axis_size("pts")
    pts_index = lax.axis_index("pts")
    full_sum = lax.dot_general(
        assign, rows, (((0,), (0,)), ((), ())), preferred_element_type=jnp.float32
    )
    total = lax.psum(full_sum, "pts")
    moved = lax.dynamic_slice_in_dim(total, pts_index * share, share, 0)
    base = lax.dynamic_slice_in_dim(cent_unit, pts_index * share, share, 0).astype(jnp.float32)
    updated = unit_rms(base + 8.0 * moved).astype(jnp.bfloat16)
    return updated[None]


def solution(mesh):
    in_specs = (P(("pts", "own"), None), P("pts", None), P(), P(), P("own", None, None))
    out_specs = P("own", "pts", None)
    return jax.shard_map(local, mesh=mesh, in_specs=in_specs, out_specs=out_specs, check_vma=False)
```

profile of v0, /device:TPU:2, one launch (start us, length us, event | category | flops | bytes accessed | tf_op | source)
XLA Modules:
  0.0 427.6 jit_solution(10960685609570992084)
XLA Ops:
  6.5 0.0 copy-start.1
  6.5 0.0 all-gather.2.cloned.1.call-start
  6.5 1.5 fusion.12
  8.1 2.2 fusion.13
  10.3 0.0 all-gather.2.cloned.1.call-update
  10.3 0.0 all-reduce.2.cloned.1.call-start
  10.4 0.9 select_reduce_fusion.3
  11.3 0.7 add.62
  11.9 2.0 select_reduce_fusion.2
  14.0 0.7 broadcast_compare_fusion.1
  14.6 0.2 fusion.16
  14.8 2.6 fusion.8
  17.4 0.0 copy-done.1
  17.4 2.3 fusion.9
  19.7 36.2 %all-gather.2.cloned.1.call-done = bf16[2048,1536]{1,0:T(8,128)(2,1)} async-done(((bf16[256,1536]{1,0:T(8,128)(2,1)}), bf16[2048,1536]{1,0:T(8,128)(2,1)}) %all-gather.2.cloned.1.call-update) | async-done | bytes 6291472 | tf_op jit(solution)/shard_map/all_gather | solution.py:30
  55.9 13.5 %fusion.19 = (f32[1024]{0:T(1024)S(1)}, f32[2048,1024]{1,0:T(8,128)}) fusion(bf16[2048,1536]{1,0:T(8,128)(2,1)} %all-gather.2.cloned.1.call-done, bf16[1024,1536]{1,0:T(8,128)(2,1)} %fusion.9, s32[2048]{0:T(1024)S(1)} %add.59, s32[2048]{0:T(1024)S(1)} %get-tuple-element.7, pred[2048]{0:T(1024)(128)(4,1)S(1)} %broadcast_compare_fusion), kind=kOutput, calls=%fused_computation.48 | convolution fusion | flops 6457129984 | bytes 17848320 | tf_op jit(solution)/shard_map/dot_general | solution.py:47
  69.5 75.1 %psum.21 = f32[1024]{0:T(1024)S(1)} all-reduce(f32[1024]{0:T(1024)S(1)} %get-tuple-element.8), channel_id=1, replica_groups=mesh['pts'=32,'own'=8] {'pts'}, use_global_device_ids=true, to_apply=%region_8.9 | all-reduce | flops 1024 | bytes 8192 | tf_op jit(solution)/shard_map/psum | solution.py:50
  144.6 0.0 copy-start
  144.6 4.2 divide_reduce_fusion
  148.7 1.6 copy-done
  150.3 1.3 fusion.4
  151.6 69.6 %psum.22 = f32[1024]{0:T(1024)S(1)} all-reduce(f32[1024]{0:T(1024)S(1)} %fusion.4), channel_id=1, replica_groups=mesh['pts'=32,'own'=8] {'pts'}, use_global_device_ids=true, to_apply=%region_11.12 | all-reduce | flops 1024 | bytes 8192 | tf_op jit(solution)/shard_map/psum | solution.py:50
  221.3 4.4 %fusion.5 = f32[2048]{0:T(1024)S(1)} fusion(f32[2048,1024]{1,0:T(8,128)} %get-tuple-element.9, f32[1024]{0:T(1024)S(1)} %broadcast_select_fusion.2, f32[2048]{0:T(1024)S(1)} %broadcast_select_fusion.1, f32[1024]{0:T(1024)S(1)} %broadcast_select_fusion.3), kind=kLoop, calls=%fused_computation.11 | loop fusion | flops 8386560 | bytes 8413184 | tf_op jit(solution)/shard_map/reduce_sum | solution.py:52
  225.7 13.1 %fusion.10 = f32[1024,1536]{1,0:T(8,128)} fusion(bf16[2048,1536]{1,0:T(8,128)(2,1)} %all-gather.2.cloned.1.call-done, f32[2048,1024]{1,0:T(8,128)} %get-tuple-element.9, f32[2048]{0:T(1024)S(1)} %broadcast_select_fusion, f32[1024]{0:T(1024)S(1)} %broadcast_select_fusion.2, f32[2048]{0:T(1024)S(1)} %broadcast_select_fusion.1, ...), kind=kOutput, calls=%fused_computation.18 | convolution fusion | flops 6452936704 | bytes 20996096 | tf_op jit(solution)/shard_map/dot_general | solution.py:57
  238.7 0.0 all-reduce.2.cloned.1.call-update
  238.8 179.2 %all-reduce.2.cloned.1.call-done = f32[1024,1536]{1,0:T(8,128)} async-done(((f32[1024,1536]{1,0:T(8,128)}), f32[1024,1536]{1,0:T(8,128)}) %all-reduce.2.cloned.1.call-update) | async-done | bytes 6291472 | tf_op jit(solution)/shard_map/psum | solution.py:60
  417.9 1.1 multiply_reduce_fusion
  419.1 1.7 fusion.17
  (9 shorter events, 0.1 us)
Async XLA Ops:
  6.5 10.9 %copy-start.1 = (bf16[1,1024,1536]{2,1,0:T(8,128)(2,1)S(1)}, bf16[1,1024,1536]{2,1,0:T(8,128)(2,1)}, u32[]{:S(2)}) copy-start(bf16[1,1024,1536]{2,1,0:T(8,128)(2,1)} %param.9) | copy-start | bytes 9437188
  6.5 49.4 %all-gather.2.cloned.1.call-start = ((), (), s32[]{:S(2)}) async-start(), calls=%async_computation | async-start | bytes 7077888 | tf_op jit(solution)/shard_map/all_gather | solution.py:30
  10.3 407.6 %all-reduce.2.cloned.1.call-start = ((), (), s32[]{:S(2)}) async-start(), calls=%async_computation.1 | async-start | bytes 12582912 | tf_op jit(solution)/shard_map/psum | solution.py:60
  144.6 5.8 %copy-start = (f32[2048,1024]{1,0:T(8,128)S(1)}, f32[2048,1024]{1,0:T(8,128)}, u32[]{:S(2)}) copy-start(f32[2048,1024]{1,0:T(8,128)} %get-tuple-element.9) | copy-start | bytes 25165828
Sparse Core Ops, SparseCore 0:
  10.4 45.4 all-gather.1
  238.9 179.0 all-reduce.1
where the time goes:
time: 428 us
  waiting for transfers between devices  215 us (50%)
  blocking collectives  145 us (34%)
  matrix products  26.6 us (6%)
  other arithmetic  25.7 us (6%)
  between operations  13.5 us (3%)
    psum x1, waiting for transfers between devices, local(): total = lax.psum(full_sum, 'pts')  179 us
    psum x2, blocking collectives, local(): column_sum = lax.psum(jnp.sum(weights, axis=0), 'pts')  145 us
    all_gather x1, waiting for transfers between devices, local(): rows = lax.all_gather(point_unit, 'own', axis=0, tiled=True)  36.2 us
    dot_general x1, matrix products, local(): jnp.dot(rows, cent_unit.T, preferred_element_type=jnp.float32)  13.5 us
    dot_general x1, matrix products, local(): lax.dot_general(assign, rows, (((0,), (0,)), ((), ())), preferred_element...  13.1 us
  transfers between devices with their start and end apart: 2, of which 2 were waited for; matrix products, arithmetic and copies ran while one was open for 2% of the time, Pallas kernels for 0%

commit v1 on v0

v1 whole, which is shorter than its diff:
```python
import functools

import jax
import jax.numpy as jnp
from jax import lax
from jax.experimental import pallas as pl
from jax.experimental.pallas import tpu as pltpu
from jax.sharding import PartitionSpec as P

SWEEPS = 2
CAP = 64
CORES = 2
NY = 4
MESH = pl.DeviceIdType.MESH
F32 = jnp.float32
BF16 = jnp.bfloat16

TILES = (
    ("yz", 0, 256, 1),
    ("zy", 1024, 256, 1),
    ("yz", 256, 256, -1),
    ("yz", 512, 256, 1),
    ("zy", 1280, 256, -1),
    ("yz", 768, 256, -1),
)


def unit_rms(values):
    values = values.astype(F32)
    return values * lax.rsqrt(jnp.mean(values * values, axis=-1, keepdims=True) + 1e-06)


def iota(shape, dim):
    return lax.broadcasted_iota(jnp.int32, shape, dim).astype(F32)


def kernel(
    ny, nz, nx,
    points_ref, parent_ref, owner_ref, count_ref, cent_hbm, out_ref,
    cent_raw, cent_unit, point_unit, packed, rows, member, onehot, place, weights, assign_t, part, final,
    ysum_send, ysum_recv, zsum_send, zsum_recv, tile_bufs,
    cent_sem, x_send, x_recv, ys_send, ys_recv, zs_send, zs_recv, rs_send, rs_recv,
):
    pts, me = lax.axis_index("pts"), lax.axis_index("own")
    y, z = lax.div(pts, nz), lax.rem(pts, nz)
    x, core = lax.div(me, CORES), lax.rem(me, CORES)
    groups = nx * CORES
    width = points_ref.shape[1]
    tokens = points_ref.shape[0]
    parents = owner_ref.shape[1]
    slots = cent_hbm.shape[0]

    def own_at(dx, dc, sign):
        other = lax.rem(x + (dx if sign > 0 else nx - dx), nx)
        return other * CORES + (core if dc == 0 else 1 - core)

    def at_y(step):
        return lax.rem(y + step + ny, ny)

    def at_z(step):
        return lax.rem(z + step + nz, nz)

    def dev_y(step):
        return (at_y(step) * nz + z, me)

    def dev_z(step):
        return (y * nz + at_z(step), me)

    offsets = [(dx, dc) for dx in range(nx) for dc in range(CORES)]
    barrier = pltpu.get_barrier_semaphore()
    peers = [(pts, own_at(dx, dc, 1)) for dx, dc in offsets if (dx, dc) != (0, 0)]
    peers += [dev_y(s) for s in range(1, ny)] + [dev_z(s) for s in range(1, nz)]
    for peer in peers:
        pl.semaphore_signal(barrier, inc=1, device_id=peer, device_id_type=MESH)
    cent_copy = pltpu.make_async_copy(cent_hbm, cent_raw, cent_sem)
    cent_copy.start()

    pending = []

    def send(src, dst, send_sem, recv_sem, device):
        copy = pltpu.make_async_remote_copy(
            src_ref=src, dst_ref=dst, send_sem=send_sem, recv_sem=recv_sem,
            device_id=device, device_id_type=MESH,
        )
        copy.start()
        pending.append(copy)
        return copy

    square = (parents, parents)
    owner_row = owner_ref[...].astype(F32)
    count_row = count_ref[...].astype(F32)
    diagonal = iota(square, 0) == iota(square, 1)
    owner_col = jnp.sum(jnp.where(diagonal, owner_row, 0.0), axis=1, keepdims=True)
    count_col = jnp.sum(jnp.where(diagonal, count_row, 0.0), axis=1, keepdims=True)
    upper = jnp.where(iota((tokens, tokens), 0) <= iota((tokens, tokens), 1), 1.0, 0.0).astype(BF16)
    parent_iota = iota((parents, tokens), 0)

    def owners_of_block(index):
        parent = parent_ref[pl.ds(index, 1), :].astype(F32)
        return parent, jnp.sum(jnp.where(parent_iota == parent, owner_col, 0.0), axis=0, keepdims=True)

    _, my_owner = owners_of_block(me)
    goes = my_owner == iota((groups, tokens), 0)
    rank = jnp.dot(jnp.where(goes, 1.0, 0.0).astype(BF16), upper, preferred_element_type=F32)
    place[...] = jnp.where(goes, rank - 1.0, -1.0)
    point_unit[...] = unit_rms(points_ref[...]).astype(BF16)

    slot_iota = iota((CAP, tokens), 0)

    def pack(group):
        picks = [
            jnp.where(place[pl.ds(own_at(dx, dc, 1), 1), :] == slot_iota, 1.0, 0.0).astype(BF16) for dx, dc in group
        ]
        return jnp.dot(jnp.concatenate(picks, axis=0), point_unit[...], preferred_element_type=F32).astype(BF16)

    far = [(dx, dc) for dx in range(nx // 2, nx // 2 + 1) for dc in range(CORES)]
    near = [(dx, dc) for dx in (1, nx - 1) for dc in range(CORES)]
    here = [(0, 1), (0, 0)]
    block_of = {offset: i for i, offset in enumerate(here + near + far)}
    arrivals = {}
    waited = False
    for group in (far, near, here):
        block = pack(group)
        for i, (dx, dc) in enumerate(group):
            k = block_of[dx, dc]
            value = block[i * CAP:(i + 1) * CAP]
            if (dx, dc) == (0, 0):
                rows[pl.ds(k * CAP, CAP), :] = value
            else:
                packed[pl.ds(k * CAP, CAP), :] = value
        if not waited:
            pl.semaphore_wait(barrier, len(peers))
            waited = True
        for dx, dc in group:
            k = block_of[dx, dc]
            if (dx, dc) != (0, 0):
                span = pl.ds(k * CAP, CAP)
                arrivals[k] = send(
                    packed.at[span], rows.at[span], x_send.at[k], x_recv.at[k], (pts, own_at(dx, dc, 1))
                )

    first_col = jnp.sum(
        jnp.where((owner_col == owner_row) & (iota(square, 1) < iota(square, 0)), count_row, 0.0),
        axis=1, keepdims=True,
    )
    my_index = me.astype(F32)
    slot_row = iota((parents, slots), 1)
    member[...] = jnp.where(
        (owner_col == my_index) & (slot_row >= first_col) & (slot_row < first_col + count_col), 1.0, 0.0
    ).astype(BF16)
    block_parent, block_live = [], []
    for dx, dc in here + near + far:
        parent, owner = owners_of_block(own_at(dx, dc, -1))
        block_parent.append(parent)
        block_live.append(owner == my_index)
    live = jnp.concatenate([jnp.where(one, 1.0, 0.0) for one in block_live], axis=0)
    rank = jnp.dot(live.astype(BF16), upper, preferred_element_type=F32)
    spot = jnp.where(live > 0.5, rank - 1.0, -1.0)
    for k in range(groups):
        chosen = spot[k:k + 1, :] == slot_iota
        parent = jnp.sum(jnp.where(chosen, block_parent[k] + 1.0, 0.0), axis=1, keepdims=True) - 1.0
        onehot[k * CAP:(k + 1) * CAP, :] = jnp.where(parent == iota((CAP, parents), 1), 1.0, 0.0).astype(BF16)

    cent_copy.wait()
    step_rows = 64

    @pl.loop(0, slots // step_rows)
    def _(i):
        span = pl.ds(pl.multiple_of(i * step_rows, step_rows), step_rows)
        cent_unit[span, :] = unit_rms(cent_raw[span, :]).astype(BF16)

    half = groups // 2
    tall = half * CAP
    scale = 1.0 / (width * 0.05)
    wide = 256
    sums = [None] * (slots // wide)
    for h in range(2):
        for k in range(h * half, (h + 1) * half):
            if k in arrivals:
                arrivals[k].wait_recv()
        span = slice(h * tall, (h + 1) * tall)
        for n in range(slots // wide):
            cols = slice(n * wide, (n + 1) * wide)
            score = lax.dot_general(
                rows[span, :], cent_unit[cols, :], (((1,), (1,)), ((), ())), preferred_element_type=F32
            )
            allowed = jnp.dot(onehot[span, :], member[:, cols], preferred_element_type=F32)
            value = jnp.where(allowed > 0.5, jnp.exp(score * scale), 0.0)
            weights[span, cols] = value
            total = jnp.sum(value, axis=0, keepdims=True)
            sums[n] = total if h == 0 else sums[n] + total
    column = jnp.concatenate(sums, axis=1)

    def column_total(sweep, local):
        ysum_send[sweep] = local
        copies = [
            send(ysum_send.at[sweep], ysum_recv.at[sweep, s - 1], ys_send.at[sweep, s - 1],
                 ys_recv.at[sweep, s - 1], dev_y(s))
            for s in range(1, ny)
        ]
        total = local
        for s, copy in enumerate(copies):
            copy.wait_recv()
            total = total + ysum_recv[sweep, s]
        zsum_send[sweep] = total
        copies = [
            send(zsum_send.at[sweep], zsum_recv.at[sweep, s - 1], zs_send.at[sweep, s - 1],
                 zs_recv.at[sweep, s - 1], dev_z(s))
            for s in range(1, nz)
        ]
        for s, copy in enumerate(copies):
            copy.wait_recv()
            total = total + zsum_recv[sweep, s]
        return total

    row_step = 128
    for sweep in range(SWEEPS):
        total = column_total(sweep, column)
        inverse = 1.0 / jnp.where(total > 0.0, total, 1.0)
        column = None
        for i in range(groups * CAP // row_step):
            span = slice(i * row_step, (i + 1) * row_step)
            value = weights[span, :] * inverse
            row_sum = jnp.sum(value, axis=1, keepdims=True)
            value = value * (1.0 / jnp.where(row_sum > 0.0, row_sum, 1.0))
            if sweep < SWEEPS - 1:
                weights[span, :] = value
                partial = jnp.sum(value, axis=0, keepdims=True)
                column = partial if column is None else column + partial
            else:
                assign_t[:, span] = jnp.transpose(value).astype(BF16)

    share = slots // (ny * nz)
    sem_base = 0
    tasks = []
    buf_at = 0
    for index, (order, first, cols, long) in enumerate(TILES):
        counts = [(ny if a == "y" else nz) - 1 for a in order]
        bufs = tile_bufs[buf_at:buf_at + 5]
        buf_at += 5
        tasks.append((index, order, first, cols, long, sem_base, bufs))
        sem_base += sum(counts)

    def run_tile(order, first, cols, long, base, bufs):
        send1, recv1, middle, send2, recv2 = bufs
        window = pl.ds(first, cols)

        def ring(axis, own_chunk, send_buf, recv_buf, sems):
            n = ny if axis == "y" else nz
            at, dev = (at_y, dev_y) if axis == "y" else (at_z, dev_z)
            far_steps, near_steps = n // 2, n // 2 - 1
            got = {}
            for t in range(1, far_steps + 1):
                for name, direction, steps, offset in (
                    ("far", long, far_steps, 0), ("near", -long, near_steps, far_steps)
                ):
                    if t > steps:
                        continue
                    slot = offset + t - 1
                    value = own_chunk(at(direction * (steps - t + 1)))
                    if t > 1:
                        got[name].wait_recv()
                        value = value + recv_buf[slot - 1].astype(F32)
                    send_buf[slot] = value.astype(BF16)
                    got[name] = send(
                        send_buf.at[slot], recv_buf.at[slot], rs_send.at[sems + slot], rs_recv.at[sems + slot],
                        dev(direction),
                    )
                yield
            value = own_chunk(at(0))
            for name, slot in (("far", far_steps - 1), ("near", n - 2)):
                if name in got:
                    got[name].wait_recv()
                    value = value + recv_buf[slot].astype(F32)
            result.append(value)

        product = jnp.dot(assign_t[...], rows[:, first:first + cols], preferred_element_type=F32)
        part[:, :, :, first:first + cols] = product.reshape(ny, nz, share, cols)
        result = []
        if order[0] == "y":
            yield from ring("y", lambda k: part[pl.ds(k, 1), :, :, window][0], send1, recv1, base)
        else:
            yield from ring("z", lambda k: part[:, pl.ds(k, 1), :, window][:, 0], send1, recv1, base)
        middle[...] = result.pop()
        base2 = base + (ny if order[0] == "y" else nz) - 1
        yield from ring(order[1], lambda k: middle[pl.ds(k, 1)][0], send2, recv2, base2)
        final[:, first:first + cols] = result.pop()

    running = []
    waiting = list(tasks)
    while running or waiting:
        if waiting:
            _, order, first, cols, long, base, bufs = waiting.pop(0)
            running.append(run_tile(order, first, cols, long, base, bufs))
        alive = []
        for one in running:
            try:
                next(one)
                alive.append(one)
            except StopIteration:
                pass
        running = alive

    base = cent_unit[pl.ds(pl.multiple_of(pts * share, share), share), :].astype(F32)
    out_ref[...] = unit_rms(base + 8.0 * final[...]).astype(BF16)
    for copy in pending:
        copy.wait_send()


def local(mesh_pts, mesh_own, points, parent_of, owner_of, child_count, centroids):
    ny = NY
    nz = mesh_pts // ny
    nx = mesh_own // CORES
    tokens, width = points.shape
    slots = centroids.shape[1]
    parents = owner_of.shape[0]
    share = slots // mesh_pts
    groups = mesh_own
    tile_shapes = []
    sems = 0
    for order, first, cols, long in TILES:
        n1, n2 = (ny, nz) if order == "yz" else (nz, ny)
        tile_shapes += [
            pltpu.VMEM((n1 - 1, n2, share, cols), BF16),
            pltpu.VMEM((n1 - 1, n2, share, cols), BF16),
            pltpu.VMEM((n2, share, cols), F32),
            pltpu.VMEM((n2 - 1, share, cols), BF16),
            pltpu.VMEM((n2 - 1, share, cols), BF16),
        ]
        sems += n1 + n2 - 2
    dma = pltpu.SemaphoreType.DMA
    out = pl.pallas_call(
        functools.partial(kernel_entry, ny, nz, nx, len(tile_shapes)),
        out_shape=jax.ShapeDtypeStruct((share, width), BF16),
        in_specs=[pl.BlockSpec(memory_space=pltpu.VMEM)] * 4 + [pl.BlockSpec(memory_space=pl.ANY)],
        out_specs=pl.BlockSpec(memory_space=pltpu.VMEM),
        scratch_shapes=[
            pltpu.VMEM((slots, width), BF16),
            pltpu.VMEM((slots, width), BF16),
            pltpu.VMEM((tokens, width), BF16),
            pltpu.VMEM((groups * CAP, width), BF16),
            pltpu.VMEM((groups * CAP, width), BF16),
            pltpu.VMEM((parents, slots), BF16),
            pltpu.VMEM((groups * CAP, parents), BF16),
            pltpu.VMEM((groups, tokens), F32),
            pltpu.VMEM((groups * CAP, slots), F32),
            pltpu.VMEM((slots, groups * CAP), BF16),
            pltpu.VMEM((ny, nz, share, width), F32),
            pltpu.VMEM((share, width), F32),
            pltpu.VMEM((SWEEPS, 1, slots), F32),
            pltpu.VMEM((SWEEPS, ny - 1, 1, slots), F32),
            pltpu.VMEM((SWEEPS, 1, slots), F32),
            pltpu.VMEM((SWEEPS, nz - 1, 1, slots), F32),
            *tile_shapes,
            dma,
            dma((groups,)),
            dma((groups,)),
            dma((SWEEPS, ny - 1)),
            dma((SWEEPS, ny - 1)),
            dma((SWEEPS, nz - 1)),
            dma((SWEEPS, nz - 1)),
            dma((sems,)),
            dma((sems,)),
        ],
        compiler_params=pltpu.CompilerParams(
            collective_id=0, has_side_effects=True, vmem_limit_bytes=60 * 1024 * 1024
        ),
    )(
        points,
        parent_of.reshape(groups, tokens),
        owner_of.reshape(1, parents),
        child_count.reshape(1, parents),
        centroids[0],
    )
    return out[None]


def kernel_entry(ny, nz, nx, tiles, *refs):
    head, rest = refs[:6 + 16], refs[6 + 16:]
    return kernel(ny, nz, nx, *head, rest[:tiles], *rest[tiles:])


def solution(mesh):
    in_specs = (P(("pts", "own"), None), P("pts", None), P(), P(), P("own", None, None))
    out_specs = P("own", "pts", None)
    body = functools.partial(local, mesh.shape["pts"], mesh.shape["own"])
    return jax.shard_map(body, mesh=mesh, in_specs=in_specs, out_specs=out_specs, check_vma=False)
```

time: 428 us -> 103 us (0.24)
  the two profiles are of different devices: /device:TPU:2 before, /device:TPU:16 now
where the time goes in v1:
time: 103 us
  Pallas kernels  98.8 us (96%)
  local copies, waits for them, and re-layouts  2.65 us (3%)
  other arithmetic  1.36 us (1%)
    pallas_call x1, Pallas kernels, local(): pl.pallas_call(functools.partial(kernel_entry, ny, nz, nx, len(tile_shape...  98.8 us

profile of v1, /device:TPU:16, one launch (start us, length us, event | category | flops | bytes accessed | tf_op | source)
XLA Modules:
  0.0 102.9 jit_solution(9870917761197719982)
XLA Ops:
  0.0 0.5 broadcast.3
  0.5 1.4 %reduce.3 = s32[2048]{0:T(1024)S(1)} reduce(s32[2048,1]{0,1:T(1,128)} %param.6, s32[]{:T(128)} %broadcast.3), dimensions={1}, to_apply=%param.6.reduce_sub_computation.3 | reduce | bytes 16388 | tf_op args[1]
  1.9 0.6 reshape.9.refs_1_
  2.5 98.8 %shard_map.55 = bf16[32,1536]{1,0:T(8,128)(2,1)} custom-call(bf16[256,1536]{1,0:T(8,128)(2,1)} %refs_0_.1, s32[8,256]{1,0:T(8,128)} %reshape.9.refs_1_, s32[1,128]{1,0:T(1,128)} %bitcast.7, s32[1,128]{1,0:T(1,128)} %bitcast.8, bf16[1024,1536]{1,0:T(8,128)(2,1)} %bitcast.5), custom_call_target="tpu_custom_call" | custom-call | tf_op jit(solution)/shard_map/pallas_call | solution.py:332
  101.3 1.5 %copy.7 = bf16[1,32,1536]{2,1,0:T(8,128)(2,1)} copy(bf16[1,32,1536]{2,1,0:T(8,128)(2,1)} %bitcast.6) | data formatting | bytes 196608

commit v2 on v1

--- a/solution.py
+++ b/solution.py
@@ -16,13 +16,96 @@
 BF16 = jnp.bfloat16
 
 TILES = (
-    ("yz", 0, 256, 1),
-    ("zy", 1024, 256, 1),
-    ("yz", 256, 256, -1),
-    ("yz", 512, 256, 1),
-    ("zy", 1280, 256, -1),
-    ("yz", 768, 256, -1),
+    ("yz", 256, -1, "direct"),
+    ("zy", 128, 1, "ring"),
+    ("yz", 128, 1, "ring"),
+    ("yz", 256, 1, "direct"),
+    ("zy", 128, -1, "direct"),
+    ("zy", 128, 1, "direct"),
+    ("zy", 128, 1, "direct"),
+    ("zy", 128, -1, "ring"),
+    ("zy", 128, -1, "direct"),
+    ("yz", 128, -1, "ring"),
 )
+
+
+def stage_messages(mode, n, long):
+    far = n // 2
+    if mode == "ring":
+        return [("far", t, long, 1) for t in range(1, far + 1)] + [("near", t, -long, 1) for t in range(1, far)]
+    return [("one", long * far, long, far)] + [
+        ("one", hops * way, way, hops) for hops in range(far - 1, 0, -1) for way in (long, -long)
+    ]
+
+
+def tile_tasks(index, tile, sizes, slots):
+    order, cols, long, mode = tile
+    share = slots
+    for axis in order:
+        share //= sizes[axis]
+    tasks = {(index, "product"): ((), (), cols * 0.0027, ())}
+    before = (index, "product")
+    for stage, axis in enumerate(order):
+        n = sizes[axis]
+        chunk = (slots // n if stage == 0 else share) * cols
+        work = chunk * 1.8e-6
+        kind = "ring" if stage == 0 else mode
+        messages = stage_messages(kind, n, long)
+        names = [(index, stage, name, step) for name, step, _, _ in messages]
+        wire = [(name, axis, way, hops, chunk * 2) for name, (_, _, way, hops) in zip(names, messages)]
+        done = (index, stage, "sum")
+        if kind == "ring":
+            for key, one in zip(names, wire):
+                last = key[:3] + (key[3] - 1,)
+                first = key[3] == 1
+                tasks[key] = ((before,) if first else (last,), () if first else (last,), work, (one,))
+            ends = [(index, stage, "far", n // 2)] + ([(index, stage, "near", n // 2 - 1)] if n > 2 else [])
+            tasks[done] = (tuple(ends), tuple(ends), 2 * work, ())
+        else:
+            tasks[index, stage, "all"] = ((before,), (), n * work, tuple(wire))
+            tasks[done] = (((index, stage, "all"),), tuple(names), n * work, ())
+        before = done
+    return tasks
+
+
+def schedule(sizes, slots):
+    rate, hop_us, next_hop_us = 46500.0, 1.9, 0.75
+    tasks = {}
+    for index, tile in enumerate(TILES):
+        tasks.update(tile_tasks(index, tile, sizes, slots))
+    sender = {message[0]: key for key, task in tasks.items() for message in task[3]}
+    after = {key: [] for key in tasks}
+    for key, (before, waits, _, _) in tasks.items():
+        for one in before:
+            after[one].append((key, 0.0))
+        for one in waits:
+            after[sender[one]].append((key, hop_us))
+    chain = {}
+
+    def length(key):
+        if key not in chain:
+            chain[key] = tasks[key][2] + max([gap + length(one) for one, gap in after[key]], default=0.0)
+        return chain[key]
+
+    now, order, arrival, link_free, done = 0.0, [], {}, {}, set()
+    while len(order) < len(tasks):
+        ready = []
+        for key, (before, waits, _, _) in tasks.items():
+            if key not in done and all(one in done for one in before) and all(one in arrival for one in waits):
+                ready.append((max([arrival[one] for one in waits], default=0.0), key))
+        started = [one for one in ready if one[0] <= now]
+        if started:
+            at, key = max(started, key=lambda one: length(one[1]))
+        else:
+            at, key = min(ready, key=lambda one: (one[0], -length(one[1])))
+        now = max(now, at) + tasks[key][2]
+        for name, axis, way, hops, size in tasks[key][3]:
+            start = max(now, link_free.get((axis, way), 0.0))
+            link_free[axis, way] = start + hops * size / rate
+            arrival[name] = link_free[axis, way] + hop_us + next_hop_us * (hops - 1)
+        done.add(key)
+        order.append(key)
+    return order
 
 
 def unit_rms(values):
@@ -96,7 +179,7 @@
     parent_iota = iota((parents, tokens), 0)
 
     def owners_of_block(index):
-        parent = parent_ref[pl.ds(index, 1), :].astype(F32)
+        parent = parent_ref[:, pl.ds(pl.multiple_of(index * tokens, tokens), tokens)].astype(F32)
         return parent, jnp.sum(jnp.where(parent_iota == parent, owner_col, 0.0), axis=0, keepdims=True)
 
     _, my_owner = owners_of_block(me)
@@ -116,7 +199,7 @@
     far = [(dx, dc) for dx in range(nx // 2, nx // 2 + 1) for dc in range(CORES)]
     near = [(dx, dc) for dx in (1, nx - 1) for dc in range(CORES)]
     here = [(0, 1), (0, 0)]
-    block_of = {offset: i for i, offset in enumerate(here + near + far)}
+    block_of = {offset: i for i, offset in enumerate(here + far + near)}
     arrivals = {}
     waited = False
     for group in (far, near, here):
@@ -149,7 +232,7 @@
         (owner_col == my_index) & (slot_row >= first_col) & (slot_row < first_col + count_col), 1.0, 0.0
     ).astype(BF16)
     block_parent, block_live = [], []
-    for dx, dc in here + near + far:
+    for dx, dc in here + far + near:
         parent, owner = owners_of_block(own_at(dx, dc, -1))
         block_parent.append(parent)
         block_live.append(owner == my_index)
@@ -231,75 +314,85 @@
                 assign_t[:, span] = jnp.transpose(value).astype(BF16)
 
     share = slots // (ny * nz)
-    sem_base = 0
-    tasks = []
-    buf_at = 0
-    for index, (order, first, cols, long) in enumerate(TILES):
-        counts = [(ny if a == "y" else nz) - 1 for a in order]
-        bufs = tile_bufs[buf_at:buf_at + 5]
-        buf_at += 5
-        tasks.append((index, order, first, cols, long, sem_base, bufs))
-        sem_base += sum(counts)
-
-    def run_tile(order, first, cols, long, base, bufs):
-        send1, recv1, middle, send2, recv2 = bufs
+    sizes = {"y": ny, "z": nz}
+    places = {"y": (at_y, dev_y), "z": (at_z, dev_z)}
+    steps, copies = {}, {}
+    first, sem = 0, 0
+    for index, (order, cols, long, mode) in enumerate(TILES):
+        send1, recv1, middle, send2, recv2 = tile_bufs[5 * index:5 * index + 5]
         window = pl.ds(first, cols)
 
-        def ring(axis, own_chunk, send_buf, recv_buf, sems):
-            n = ny if axis == "y" else nz
-            at, dev = (at_y, dev_y) if axis == "y" else (at_z, dev_z)
-            far_steps, near_steps = n // 2, n // 2 - 1
-            got = {}
-            for t in range(1, far_steps + 1):
-                for name, direction, steps, offset in (
-                    ("far", long, far_steps, 0), ("near", -long, near_steps, far_steps)
-                ):
-                    if t > steps:
-                        continue
-                    slot = offset + t - 1
-                    value = own_chunk(at(direction * (steps - t + 1)))
-                    if t > 1:
-                        got[name].wait_recv()
-                        value = value + recv_buf[slot - 1].astype(F32)
-                    send_buf[slot] = value.astype(BF16)
-                    got[name] = send(
-                        send_buf.at[slot], recv_buf.at[slot], rs_send.at[sems + slot], rs_recv.at[sems + slot],
-                        dev(direction),
-                    )
-                yield
-            value = own_chunk(at(0))
-            for name, slot in (("far", far_steps - 1), ("near", n - 2)):
-                if name in got:
-                    got[name].wait_recv()
-                    value = value + recv_buf[slot].astype(F32)
-            result.append(value)
-
-        product = jnp.dot(assign_t[...], rows[:, first:first + cols], preferred_element_type=F32)
-        part[:, :, :, first:first + cols] = product.reshape(ny, nz, share, cols)
-        result = []
-        if order[0] == "y":
-            yield from ring("y", lambda k: part[pl.ds(k, 1), :, :, window][0], send1, recv1, base)
-        else:
-            yield from ring("z", lambda k: part[:, pl.ds(k, 1), :, window][:, 0], send1, recv1, base)
-        middle[...] = result.pop()
-        base2 = base + (ny if order[0] == "y" else nz) - 1
-        yield from ring(order[1], lambda k: middle[pl.ds(k, 1)][0], send2, recv2, base2)
-        final[:, first:first + cols] = result.pop()
-
-    running = []
-    waiting = list(tasks)
-    while running or waiting:
-        if waiting:
-            _, order, first, cols, long, base, bufs = waiting.pop(0)
-            running.append(run_tile(order, first, cols, long, base, bufs))
-        alive = []
-        for one in running:
-            try:
-                next(one)
-                alive.append(one)
-            except StopIteration:
-                pass
-        running = alive
+        def product(window=window, first=first, cols=cols):
+            value = jnp.dot(assign_t[...], rows[:, first:first + cols], preferred_element_type=F32)
+            part[:, :, :, first:first + cols] = value.reshape(ny, nz, share, cols)
+
+        steps[index, "product"] = product
+        for stage, axis in enumerate(order):
+            n = sizes[axis]
+            at, dev = places[axis]
+            kind = "ring" if stage == 0 else mode
+            send_buf, recv_buf = (send1, recv1) if stage == 0 else (send2, recv2)
+            if stage == 1:
+                def chunk(k, middle=middle):
+                    return middle[pl.ds(k, 1)][0]
+            elif axis == "y":
+                def chunk(k, window=window):
+                    return part[pl.ds(k, 1), :, :, window][0]
+            else:
+                def chunk(k, window=window):
+                    return part[:, pl.ds(k, 1), :, window][:, 0]
+
+            messages = stage_messages(kind, n, long)
+            names = [(index, stage, name, step) for name, step, _, _ in messages]
+            slot_of = {name: slot for slot, name in enumerate(names)}
+
+            def put(key, value, device, slot_of=slot_of, send_buf=send_buf, recv_buf=recv_buf, sem=sem):
+                slot = slot_of[key]
+                send_buf[slot] = value.astype(BF16)
+                copies[key] = send(
+                    send_buf.at[slot], recv_buf.at[slot], rs_send.at[sem + slot], rs_recv.at[sem + slot], device
+                )
+
+            def got(key, slot_of=slot_of, recv_buf=recv_buf):
+                copies[key].wait_recv()
+                return recv_buf[slot_of[key]].astype(F32)
+
+            def total(keys, at=at, chunk=chunk, got=got, stage=stage, middle=middle, first=first, cols=cols):
+                value = chunk(at(0))
+                for key in keys:
+                    value = value + got(key)
+                if stage == 0:
+                    middle[...] = value
+                else:
+                    final[:, first:first + cols] = value
+
+            if kind == "ring":
+                for key, (name, step, way, _) in zip(names, messages):
+                    last = n // 2 if name == "far" else n // 2 - 1
+
+                    def forward(
+                        key=key, step=step, way=way, last=last, at=at, dev=dev, chunk=chunk, got=got, put=put
+                    ):
+                        value = chunk(at(way * (last - step + 1)))
+                        if step > 1:
+                            value = value + got(key[:3] + (step - 1,))
+                        put(key, value, dev(way))
+
+                    steps[key] = forward
+                ends = [key for key in names if key[3] == (n // 2 if key[2] == "far" else n // 2 - 1)]
+            else:
+                def spread(names=names, at=at, dev=dev, chunk=chunk, put=put):
+                    for key in names:
+                        put(key, chunk(at(key[3])), dev(key[3]))
+
+                steps[index, stage, "all"] = spread
+                ends = names
+            steps[index, stage, "sum"] = functools.partial(total, ends)
+            sem += n - 1
+        first += cols
+
+    for key in schedule(sizes, slots):
+        steps[key]()
 
     base = cent_unit[pl.ds(pl.multiple_of(pts * share, share), share), :].astype(F32)
     out_ref[...] = unit_rms(base + 8.0 * final[...]).astype(BF16)
@@ -318,7 +411,7 @@
     groups = mesh_own
     tile_shapes = []
     sems = 0
-    for order, first, cols, long in TILES:
+    for order, cols, _, _ in TILES:
         n1, n2 = (ny, nz) if order == "yz" else (nz, ny)
         tile_shapes += [
             pltpu.VMEM((n1 - 1, n2, share, cols), BF16),
@@ -367,7 +460,7 @@
         ),
     )(
         points,
-        parent_of.reshape(groups, tokens),
+        parent_of.reshape(1, groups * tokens),
         owner_of.reshape(1, parents),
         child_count.reshape(1, parents),
         centroids[0],

time: 103 us -> 78.3 us (0.76)
  the two profiles are of different devices: /device:TPU:16 before, /device:TPU:2 now
where the time goes in v2:
time: 78.3 us; the launch traced here: 76.8 us
  Pallas kernels  75.2 us (96%)
  local copies, waits for them, and re-layouts  1.54 us (2%)
    pallas_call x1, Pallas kernels, local(): pl.pallas_call(functools.partial(kernel_entry, ny, nz, nx, len(tile_shape...  75.2 us

profile of v2, /device:TPU:2, one launch (start us, length us, event | category | flops | bytes accessed | tf_op | source)
XLA Modules:
  0.0 76.8 jit_solution(9825616702326759842)
XLA Ops:
  0.0 75.2 %shard_map.55 = bf16[32,1536]{1,0:T(8,128)(2,1)} custom-call(bf16[256,1536]{1,0:T(8,128)(2,1)} %refs_0_.1, s32[1,2048]{1,0:T(1,128)} %bitcast.7, s32[1,128]{1,0:T(1,128)} %bitcast.8, s32[1,128]{1,0:T(1,128)} %bitcast.9, bf16[1024,1536]{1,0:T(8,128)(2,1)} %bitcast.5), custom_call_target="tpu_custom_call" | custom-call | tf_op jit(solution)/shard_map/pallas_call | solution.py:425
  75.2 1.5 %copy.7 = bf16[1,32,1536]{2,1,0:T(8,128)(2,1)} copy(bf16[1,32,1536]{2,1,0:T(8,128)(2,1)} %bitcast.6) | data formatting | bytes 196608

commit v3 on v2

--- a/solution.py
+++ b/solution.py
@@ -9,23 +9,27 @@
 
 SWEEPS = 2
 CAP = 64
+PAIR = 96
+HALF = PAIR // 2
+EXTRA = CAP - HALF
 CORES = 2
 NY = 4
 MESH = pl.DeviceIdType.MESH
 F32 = jnp.float32
 BF16 = jnp.bfloat16
 
+GROUP = 256
 TILES = (
-    ("yz", 256, -1, "direct"),
-    ("zy", 128, 1, "ring"),
-    ("yz", 128, 1, "ring"),
-    ("yz", 256, 1, "direct"),
-    ("zy", 128, -1, "direct"),
-    ("zy", 128, 1, "direct"),
-    ("zy", 128, 1, "direct"),
-    ("zy", 128, -1, "ring"),
-    ("zy", 128, -1, "direct"),
-    ("yz", 128, -1, "ring"),
+    ("yz", 0, 256, -1, "direct"),
+    ("zy", 1, 128, 1, "direct"),
+    ("zy", 1, 128, -1, "direct"),
+    ("zy", 2, 128, -1, "direct"),
+    ("zy", 2, 128, 1, "direct"),
+    ("yz", 3, 256, 1, "direct"),
+    ("yz", 4, 128, -1, "ring"),
+    ("yz", 4, 128, 1, "ring"),
+    ("zy", 5, 128, -1, "direct"),
+    ("zy", 5, 128, 1, "direct"),
 )
 
 
@@ -39,16 +43,16 @@
 
 
 def tile_tasks(index, tile, sizes, slots):
-    order, cols, long, mode = tile
+    order, group, cols, long, mode = tile
     share = slots
     for axis in order:
         share //= sizes[axis]
-    tasks = {(index, "product"): ((), (), cols * 0.0027, ())}
-    before = (index, "product")
+    before = ("product", group)
+    tasks = {before: ((), (), 0.68, ())}
     for stage, axis in enumerate(order):
         n = sizes[axis]
         chunk = (slots // n if stage == 0 else share) * cols
-        work = chunk * 1.8e-6
+        work = chunk * 2.1e-6
         kind = "ring" if stage == 0 else mode
         messages = stage_messages(kind, n, long)
         names = [(index, stage, name, step) for name, step, _, _ in messages]
@@ -69,7 +73,7 @@
 
 
 def schedule(sizes, slots):
-    rate, hop_us, next_hop_us = 46500.0, 1.9, 0.75
+    rate, hop_us, next_hop_us = 46500.0, 2.2, 0.75
     tasks = {}
     for index, tile in enumerate(TILES):
         tasks.update(tile_tasks(index, tile, sizes, slots))
@@ -119,17 +123,16 @@
 
 def kernel(
     ny, nz, nx,
-    points_ref, parent_ref, owner_ref, count_ref, cent_hbm, out_ref,
-    cent_raw, cent_unit, point_unit, packed, rows, member, onehot, place, weights, assign_t, part, final,
+    points_hbm, parent_ref, owner_ref, count_ref, cent_hbm, out_ref,
+    point_raw, cent_raw, cent_unit, point_unit, packed, rows, member, onehot, place, weights, assign_t, part, final,
     ysum_send, ysum_recv, zsum_send, zsum_recv, tile_bufs,
-    cent_sem, x_send, x_recv, ys_send, ys_recv, zs_send, zs_recv, rs_send, rs_recv,
+    point_sem, cent_sem, x_send, x_recv, f_send, f_recv, ys_send, ys_recv, zs_send, zs_recv, rs_send, rs_recv,
 ):
     pts, me = lax.axis_index("pts"), lax.axis_index("own")
     y, z = lax.div(pts, nz), lax.rem(pts, nz)
     x, core = lax.div(me, CORES), lax.rem(me, CORES)
     groups = nx * CORES
-    width = points_ref.shape[1]
-    tokens = points_ref.shape[0]
+    tokens, width = points_hbm.shape
     parents = owner_ref.shape[1]
     slots = cent_hbm.shape[0]
 
@@ -155,6 +158,8 @@
     peers += [dev_y(s) for s in range(1, ny)] + [dev_z(s) for s in range(1, nz)]
     for peer in peers:
         pl.semaphore_signal(barrier, inc=1, device_id=peer, device_id_type=MESH)
+    point_copy = pltpu.make_async_copy(points_hbm, point_raw, point_sem)
+    point_copy.start()
     cent_copy = pltpu.make_async_copy(cent_hbm, cent_raw, cent_sem)
     cent_copy.start()
 
@@ -185,42 +190,64 @@
     _, my_owner = owners_of_block(me)
     goes = my_owner == iota((groups, tokens), 0)
     rank = jnp.dot(jnp.where(goes, 1.0, 0.0).astype(BF16), upper, preferred_element_type=F32)
-    place[...] = jnp.where(goes, rank - 1.0, -1.0)
-    point_unit[...] = unit_rms(points_ref[...]).astype(BF16)
-
-    slot_iota = iota((CAP, tokens), 0)
+    odd = lax.rem(lax.broadcasted_iota(jnp.int32, (groups, tokens), 0), CORES) == 1
+    place[...] = jnp.where(goes, jnp.where(odd, PAIR - rank, rank - 1.0), -1.0)
+    point_copy.wait()
+    point_unit[...] = unit_rms(point_raw[...]).astype(BF16)
+
+    pair_iota = iota((PAIR, tokens), 0)
+    near, far = (1, nx - 1), (nx // 2,)
+    blocks = [(dx, dc) for dx in (0,) + near + far for dc in range(CORES)]
+    block_of = {offset: i for i, offset in enumerate(blocks)}
 
     def pack(group):
-        picks = [
-            jnp.where(place[pl.ds(own_at(dx, dc, 1), 1), :] == slot_iota, 1.0, 0.0).astype(BF16) for dx, dc in group
-        ]
-        return jnp.dot(jnp.concatenate(picks, axis=0), point_unit[...], preferred_element_type=F32).astype(BF16)
-
-    far = [(dx, dc) for dx in range(nx // 2, nx // 2 + 1) for dc in range(CORES)]
-    near = [(dx, dc) for dx in (1, nx - 1) for dc in range(CORES)]
-    here = [(0, 1), (0, 0)]
-    block_of = {offset: i for i, offset in enumerate(here + far + near)}
-    arrivals = {}
-    waited = False
-    for group in (far, near, here):
-        block = pack(group)
-        for i, (dx, dc) in enumerate(group):
+        picks = []
+        for dx in group:
+            chip = lax.rem(x + dx, nx) * CORES
+            taken = place[pl.ds(chip, 1), :] == pair_iota
+            for other in range(1, CORES):
+                taken = taken | (place[pl.ds(chip + other, 1), :] == pair_iota)
+            picks.append(jnp.where(taken, 1.0, 0.0).astype(BF16))
+        block = jnp.dot(jnp.concatenate(picks, axis=0), point_unit[...], preferred_element_type=F32).astype(BF16)
+        for i, dx in enumerate(group):
+            packed[dx * PAIR:(dx + 1) * PAIR, :] = block[i * PAIR:(i + 1) * PAIR]
+
+    def part_of(start, size):
+        return pl.ds(pl.multiple_of(start, EXTRA), size)
+
+    arrivals, forwards = {}, {}
+
+    def depart(dx):
+        for dc in range(CORES):
             k = block_of[dx, dc]
-            value = block[i * CAP:(i + 1) * CAP]
-            if (dx, dc) == (0, 0):
-                rows[pl.ds(k * CAP, CAP), :] = value
-            else:
-                packed[pl.ds(k * CAP, CAP), :] = value
-        if not waited:
-            pl.semaphore_wait(barrier, len(peers))
-            waited = True
-        for dx, dc in group:
-            k = block_of[dx, dc]
-            if (dx, dc) != (0, 0):
-                span = pl.ds(k * CAP, CAP)
-                arrivals[k] = send(
-                    packed.at[span], rows.at[span], x_send.at[k], x_recv.at[k], (pts, own_at(dx, dc, 1))
-                )
+            to_core = core if dc == 0 else 1 - core
+            arrivals[dx, dc] = send(
+                packed.at[part_of(dx * PAIR + HALF * to_core, HALF)], rows.at[part_of(k * CAP + EXTRA * to_core, HALF)],
+                x_send.at[k], x_recv.at[k], (pts, own_at(dx, dc, 1)),
+            )
+
+    def hand_over(dx, dc):
+        k, other = block_of[dx, dc], block_of[dx, 1 - dc]
+        arrivals[dx, dc].wait_recv()
+        forwards[dx, dc] = send(
+            rows.at[part_of(k * CAP + 2 * EXTRA - EXTRA * core, EXTRA)], rows.at[part_of(other * CAP + HALF * core, EXTRA)],
+            f_send.at[k], f_recv.at[other], (pts, own_at(0, 1, 1)),
+        )
+
+    pack(near)
+    pl.semaphore_wait(barrier, len(peers))
+    for dx in near:
+        depart(dx)
+    pack(far)
+    for dx in far:
+        depart(dx)
+    pack((0,))
+    mine, theirs = block_of[0, 0], block_of[0, 1]
+    rows[mine * CAP:(mine + 1) * CAP, :] = packed[part_of((PAIR - CAP) * core, CAP), :]
+    arrivals[0, 1] = send(
+        packed.at[part_of((PAIR - CAP) * (1 - core), CAP)], rows.at[pl.ds(theirs * CAP, CAP)],
+        x_send.at[theirs], x_recv.at[theirs], (pts, own_at(0, 1, 1)),
+    )
 
     first_col = jnp.sum(
         jnp.where((owner_col == owner_row) & (iota(square, 1) < iota(square, 0)), count_row, 0.0),
@@ -232,13 +259,15 @@
         (owner_col == my_index) & (slot_row >= first_col) & (slot_row < first_col + count_col), 1.0, 0.0
     ).astype(BF16)
     block_parent, block_live = [], []
-    for dx, dc in here + far + near:
+    for dx, dc in blocks:
         parent, owner = owners_of_block(own_at(dx, dc, -1))
         block_parent.append(parent)
         block_live.append(owner == my_index)
     live = jnp.concatenate([jnp.where(one, 1.0, 0.0) for one in block_live], axis=0)
     rank = jnp.dot(live.astype(BF16), upper, preferred_element_type=F32)
     spot = jnp.where(live > 0.5, rank - 1.0, -1.0)
+    slot_iota = iota((CAP, tokens), 0)
+    slot_iota = jnp.where(core == 0, slot_iota, (CAP - 1.0) - slot_iota)
     for k in range(groups):
         chosen = spot[k:k + 1, :] == slot_iota
         parent = jnp.sum(jnp.where(chosen, block_parent[k] + 1.0, 0.0), axis=1, keepdims=True) - 1.0
@@ -252,16 +281,21 @@
         span = pl.ds(pl.multiple_of(i * step_rows, step_rows), step_rows)
         cent_unit[span, :] = unit_rms(cent_raw[span, :]).astype(BF16)
 
-    half = groups // 2
-    tall = half * CAP
     scale = 1.0 / (width * 0.05)
     wide = 256
     sums = [None] * (slots // wide)
-    for h in range(2):
-        for k in range(h * half, (h + 1) * half):
-            if k in arrivals:
-                arrivals[k].wait_recv()
-        span = slice(h * tall, (h + 1) * tall)
+    done = 0
+    for stage in (near, far):
+        for dx in stage:
+            for dc in range(CORES):
+                hand_over(dx, dc)
+        if stage is near:
+            arrivals[0, 1].wait_recv()
+        for dx in stage:
+            for dc in range(CORES):
+                forwards[dx, dc].wait_recv()
+        ready = done + (len(stage) + (1 if stage is near else 0)) * CORES * CAP
+        span = slice(done, ready)
         for n in range(slots // wide):
             cols = slice(n * wide, (n + 1) * wide)
             score = lax.dot_general(
@@ -271,7 +305,8 @@
             value = jnp.where(allowed > 0.5, jnp.exp(score * scale), 0.0)
             weights[span, cols] = value
             total = jnp.sum(value, axis=0, keepdims=True)
-            sums[n] = total if h == 0 else sums[n] + total
+            sums[n] = total if done == 0 else sums[n] + total
+        done = ready
     column = jnp.concatenate(sums, axis=1)
 
     def column_total(sweep, local):
@@ -317,16 +352,20 @@
     sizes = {"y": ny, "z": nz}
     places = {"y": (at_y, dev_y), "z": (at_z, dev_z)}
     steps, copies = {}, {}
-    first, sem = 0, 0
-    for index, (order, cols, long, mode) in enumerate(TILES):
+    sem = 0
+    taken_columns = [group * GROUP for group in range(width // GROUP)]
+    for group in {tile[1] for tile in TILES}:
+        def product(span=slice(group * GROUP, (group + 1) * GROUP)):
+            value = jnp.dot(assign_t[...], rows[:, span], preferred_element_type=F32)
+            part[:, :, :, span] = value.reshape(ny, nz, share, GROUP)
+
+        steps["product", group] = product
+    for index, (order, group_of, cols, long, mode) in enumerate(TILES):
         send1, recv1, middle, send2, recv2 = tile_bufs[5 * index:5 * index + 5]
+        first = taken_columns[group_of]
+        taken_columns[group_of] += cols
         window = pl.ds(first, cols)
 
-        def product(window=window, first=first, cols=cols):
-            value = jnp.dot(assign_t[...], rows[:, first:first + cols], preferred_element_type=F32)
-            part[:, :, :, first:first + cols] = value.reshape(ny, nz, share, cols)
-
-        steps[index, "product"] = product
         for stage, axis in enumerate(order):
             n = sizes[axis]
             at, dev = places[axis]
@@ -389,7 +428,6 @@
                 ends = names
             steps[index, stage, "sum"] = functools.partial(total, ends)
             sem += n - 1
-        first += cols
 
     for key in schedule(sizes, slots):
         steps[key]()
@@ -411,7 +449,7 @@
     groups = mesh_own
     tile_shapes = []
     sems = 0
-    for order, cols, _, _ in TILES:
+    for order, _, cols, _, _ in TILES:
         n1, n2 = (ny, nz) if order == "yz" else (nz, ny)
         tile_shapes += [
             pltpu.VMEM((n1 - 1, n2, share, cols), BF16),
@@ -425,13 +463,16 @@
     out = pl.pallas_call(
         functools.partial(kernel_entry, ny, nz, nx, len(tile_shapes)),
         out_shape=jax.ShapeDtypeStruct((share, width), BF16),
-        in_specs=[pl.BlockSpec(memory_space=pltpu.VMEM)] * 4 + [pl.BlockSpec(memory_space=pl.ANY)],
+        in_specs=[pl.BlockSpec(memory_space=pl.ANY)]
+        + [pl.BlockSpec(memory_space=pltpu.VMEM)] * 3
+        + [pl.BlockSpec(memory_space=pl.ANY)],
         out_specs=pl.BlockSpec(memory_space=pltpu.VMEM),
         scratch_shapes=[
+            pltpu.VMEM((tokens, width), BF16),
             pltpu.VMEM((slots, width), BF16),
             pltpu.VMEM((slots, width), BF16),
             pltpu.VMEM((tokens, width), BF16),
-            pltpu.VMEM((groups * CAP, width), BF16),
+            pltpu.VMEM((nx * PAIR, width), BF16),
             pltpu.VMEM((groups * CAP, width), BF16),
             pltpu.VMEM((parents, slots), BF16),
             pltpu.VMEM((groups * CAP, parents), BF16),
@@ -446,6 +487,9 @@
             pltpu.VMEM((SWEEPS, nz - 1, 1, slots), F32),
             *tile_shapes,
             dma,
+            dma,
+            dma((groups,)),
+            dma((groups,)),
             dma((groups,)),
             dma((groups,)),
             dma((SWEEPS, ny - 1)),
@@ -469,7 +513,7 @@
 
 
 def kernel_entry(ny, nz, nx, tiles, *refs):
-    head, rest = refs[:6 + 16], refs[6 + 16:]
+    head, rest = refs[:6 + 17], refs[6 + 17:]
     return kernel(ny, nz, nx, *head, rest[:tiles], *rest[tiles:])
 
 

time: 78.3 us -> 72.7 us (0.928); the launches traced: 76.8 us -> 72.3 us
  Pallas kernels: 75.2 us -> 70.8 us
    pallas_call x1, Pallas kernels: 75.2 us -> 70.8 us  [local(): pl.pallas_call(functools.partial(kernel_entry, ny, nz, nx, len(tile_shape...]
where the time goes in v3:
time: 72.7 us; the launch traced here: 72.3 us
  Pallas kernels  70.8 us (97%)
  local copies, waits for them, and re-layouts  1.54 us (2%)
    pallas_call x1, Pallas kernels, local(): pl.pallas_call(functools.partial(kernel_entry, ny, nz, nx, len(tile_shape...  70.8 us
    unnamed x1, local copies, waits for them, and re-layouts  1.54 us

profile of v3, /device:TPU:2, one launch (start us, length us, event | category | flops | bytes accessed | tf_op | source)
XLA Modules:
  0.0 72.3 jit_solution(6919809858662904704)
XLA Ops:
  0.0 70.8 %shard_map.55 = bf16[32,1536]{1,0:T(8,128)(2,1)} custom-call(bf16[256,1536]{1,0:T(8,128)(2,1)} %refs_0_.1, s32[1,2048]{1,0:T(1,128)} %bitcast.7, s32[1,128]{1,0:T(1,128)} %bitcast.8, s32[1,128]{1,0:T(1,128)} %bitcast.9, bf16[1024,1536]{1,0:T(8,128)(2,1)} %bitcast.5), custom_call_target="tpu_custom_call" | custom-call | tf_op jit(solution)/shard_map/pallas_call | solution.py:463
  70.8 1.5 %copy.7 = bf16[1,32,1536]{2,1,0:T(8,128)(2,1)} copy(bf16[1,32,1536]{2,1,0:T(8,128)(2,1)} %bitcast.6) | data formatting | bytes 196608

commit v4 on v3

--- a/solution.py
+++ b/solution.py
@@ -12,6 +12,7 @@
 PAIR = 96
 HALF = PAIR // 2
 EXTRA = CAP - HALF
+LAST = 384
 CORES = 2
 NY = 4
 MESH = pl.DeviceIdType.MESH
@@ -125,8 +126,9 @@
     ny, nz, nx,
     points_hbm, parent_ref, owner_ref, count_ref, cent_hbm, out_ref,
     point_raw, cent_raw, cent_unit, point_unit, packed, rows, member, onehot, place, weights, assign_t, part, final,
-    ysum_send, ysum_recv, zsum_send, zsum_recv, tile_bufs,
-    point_sem, cent_sem, x_send, x_recv, f_send, f_recv, ys_send, ys_recv, zs_send, zs_recv, rs_send, rs_recv,
+    sum_send, sum_recv, tile_bufs,
+    point_sem, cent_sem, x_send, x_recv, l_send, l_recv, f_send, f_recv, s_send, s_recv, rs_send, rs_recv,
+    round_sem,
 ):
     pts, me = lax.axis_index("pts"), lax.axis_index("own")
     y, z = lax.div(pts, nz), lax.rem(pts, nz)
@@ -155,7 +157,7 @@
     offsets = [(dx, dc) for dx in range(nx) for dc in range(CORES)]
     barrier = pltpu.get_barrier_semaphore()
     peers = [(pts, own_at(dx, dc, 1)) for dx, dc in offsets if (dx, dc) != (0, 0)]
-    peers += [dev_y(s) for s in range(1, ny)] + [dev_z(s) for s in range(1, nz)]
+    peers += [dev_y(s) for s in range(1, ny)] + [dev_z(1), dev_z(-1)]
     for peer in peers:
         pl.semaphore_signal(barrier, inc=1, device_id=peer, device_id_type=MESH)
     point_copy = pltpu.make_async_copy(points_hbm, point_raw, point_sem)
@@ -197,7 +199,7 @@
 
     pair_iota = iota((PAIR, tokens), 0)
     near, far = (1, nx - 1), (nx // 2,)
-    blocks = [(dx, dc) for dx in (0,) + near + far for dc in range(CORES)]
+    blocks = [(dx, dc) for dx in (0,) + far + near for dc in range(CORES)]
     block_of = {offset: i for i, offset in enumerate(blocks)}
 
     def pack(group):
@@ -215,32 +217,54 @@
     def part_of(start, size):
         return pl.ds(pl.multiple_of(start, EXTRA), size)
 
-    arrivals, forwards = {}, {}
-
-    def depart(dx):
-        for dc in range(CORES):
-            k = block_of[dx, dc]
-            to_core = core if dc == 0 else 1 - core
-            arrivals[dx, dc] = send(
-                packed.at[part_of(dx * PAIR + HALF * to_core, HALF)], rows.at[part_of(k * CAP + EXTRA * to_core, HALF)],
-                x_send.at[k], x_recv.at[k], (pts, own_at(dx, dc, 1)),
-            )
-
-    def hand_over(dx, dc):
-        k, other = block_of[dx, dc], block_of[dx, 1 - dc]
-        arrivals[dx, dc].wait_recv()
-        forwards[dx, dc] = send(
-            rows.at[part_of(k * CAP + 2 * EXTRA - EXTRA * core, EXTRA)], rows.at[part_of(other * CAP + HALF * core, EXTRA)],
-            f_send.at[k], f_recv.at[other], (pts, own_at(0, 1, 1)),
-        )
-
+    arrivals, lasts, forwards = {}, {}, {}
+
+    early, late = slice(0, width - LAST), slice(width - LAST, width)
+
+    def depart(group):
+        for window in (early, late):
+            for dx in group:
+                for dc in range(CORES):
+                    k = block_of[dx, dc]
+                    to_core = core if dc == 0 else 1 - core
+                    device = (pts, own_at(dx, dc, 1))
+                    span = slice(0, width) if group is far else window
+                    if window is early:
+                        arrivals[dx, dc] = send(
+                            packed.at[part_of(dx * PAIR + HALF * to_core, HALF), span],
+                            rows.at[part_of(k * CAP + EXTRA * to_core, HALF), span],
+                            x_send.at[k], x_recv.at[k], device,
+                        )
+                    elif group is near:
+                        lasts[dx, dc] = send(
+                            packed.at[part_of(dx * PAIR + (PAIR - CAP) * to_core, CAP), span],
+                            rows.at[pl.ds(k * CAP, CAP), span],
+                            l_send.at[k], l_recv.at[k], device,
+                        )
+
+    def hand_over(group, span):
+        for dx in group:
+            for dc in range(CORES):
+                k, other = block_of[dx, dc], block_of[dx, 1 - dc]
+                arrivals[dx, dc].wait_recv()
+                forwards[dx, dc] = send(
+                    rows.at[part_of(k * CAP + 2 * EXTRA - EXTRA * core, EXTRA), span],
+                    rows.at[part_of(other * CAP + HALF * core, EXTRA), span],
+                    f_send.at[k], f_recv.at[other], (pts, own_at(0, 1, 1)),
+                )
+
+    def handed_over(group):
+        for dx in group:
+            for dc in range(CORES):
+                forwards[dx, dc].wait_recv()
+
+    pack(far)
+    pl.semaphore_wait(barrier, len(peers))
+    for step in (1, -1):
+        pl.semaphore_signal(round_sem.at[0], inc=1, device_id=dev_z(step), device_id_type=MESH)
+    depart(far)
     pack(near)
-    pl.semaphore_wait(barrier, len(peers))
-    for dx in near:
-        depart(dx)
-    pack(far)
-    for dx in far:
-        depart(dx)
+    depart(near)
     pack((0,))
     mine, theirs = block_of[0, 0], block_of[0, 1]
     rows[mine * CAP:(mine + 1) * CAP, :] = packed[part_of((PAIR - CAP) * core, CAP), :]
@@ -281,54 +305,62 @@
         span = pl.ds(pl.multiple_of(i * step_rows, step_rows), step_rows)
         cent_unit[span, :] = unit_rms(cent_raw[span, :]).astype(BF16)
 
+    pl.semaphore_wait(round_sem.at[0], 2)
+    for step in (2, -2):
+        pl.semaphore_signal(round_sem.at[1], inc=1, device_id=dev_z(step), device_id_type=MESH)
+
     scale = 1.0 / (width * 0.05)
     wide = 256
-    sums = [None] * (slots // wide)
-    done = 0
-    for stage in (near, far):
-        for dx in stage:
-            for dc in range(CORES):
-                hand_over(dx, dc)
-        if stage is near:
-            arrivals[0, 1].wait_recv()
-        for dx in stage:
-            for dc in range(CORES):
-                forwards[dx, dc].wait_recv()
-        ready = done + (len(stage) + (1 if stage is near else 0)) * CORES * CAP
-        span = slice(done, ready)
-        for n in range(slots // wide):
-            cols = slice(n * wide, (n + 1) * wide)
-            score = lax.dot_general(
-                rows[span, :], cent_unit[cols, :], (((1,), (1,)), ((), ())), preferred_element_type=F32
-            )
-            allowed = jnp.dot(onehot[span, :], member[:, cols], preferred_element_type=F32)
-            value = jnp.where(allowed > 0.5, jnp.exp(score * scale), 0.0)
-            weights[span, cols] = value
-            total = jnp.sum(value, axis=0, keepdims=True)
-            sums[n] = total if done == 0 else sums[n] + total
-        done = ready
+
+    def score(span, cols, depth):
+        return lax.dot_general(
+            rows[span, depth], cent_unit[cols, depth], (((1,), (1,)), ((), ())), preferred_element_type=F32
+        )
+
+    def weigh(span, cols, value):
+        allowed = jnp.dot(onehot[span, :], member[:, cols], preferred_element_type=F32)
+        value = jnp.where(allowed > 0.5, jnp.exp(value * scale), 0.0)
+        weights[span, cols] = value
+        return jnp.sum(value, axis=0, keepdims=True)
+
+    first_rows = (1 + len(far)) * CORES * CAP
+    top, bottom = slice(0, first_rows), slice(first_rows, groups * CAP)
+    slot_cols = [slice(n * wide, (n + 1) * wide) for n in range(slots // wide)]
+    arrivals[0, 1].wait_recv()
+    hand_over(far, slice(0, width))
+    handed_over(far)
+    sums = [weigh(top, cols, score(top, cols, slice(0, width))) for cols in slot_cols]
+    pl.semaphore_wait(round_sem.at[1], 2)
+    for step in (1, -1):
+        pl.semaphore_signal(round_sem.at[2], inc=1, device_id=dev_z(step), device_id_type=MESH)
+    hand_over(near, early)
+    handed_over(near)
+    for cols in slot_cols:
+        weights[bottom, cols] = score(bottom, cols, early)
+    for dx in near:
+        for dc in range(CORES):
+            lasts[dx, dc].wait_recv()
+    for n, cols in enumerate(slot_cols):
+        sums[n] = sums[n] + weigh(bottom, cols, weights[bottom, cols] + score(bottom, cols, late))
     column = jnp.concatenate(sums, axis=1)
+    pl.semaphore_wait(round_sem.at[2], 2)
+
+    plane = sorted(
+        ((dy, dz) for dy in range(ny) for dz in range(nz) if (dy, dz) != (0, 0)),
+        key=lambda one: -min(one[0], ny - one[0]) - min(one[1], nz - one[1]),
+    )
 
     def column_total(sweep, local):
-        ysum_send[sweep] = local
+        sum_send[sweep] = local
         copies = [
-            send(ysum_send.at[sweep], ysum_recv.at[sweep, s - 1], ys_send.at[sweep, s - 1],
-                 ys_recv.at[sweep, s - 1], dev_y(s))
-            for s in range(1, ny)
+            send(sum_send.at[sweep], sum_recv.at[sweep, k], s_send.at[sweep, k], s_recv.at[sweep, k],
+                 (at_y(dy) * nz + at_z(dz), me))
+            for k, (dy, dz) in enumerate(plane)
         ]
         total = local
-        for s, copy in enumerate(copies):
+        for k, copy in reversed(list(enumerate(copies))):
             copy.wait_recv()
-            total = total + ysum_recv[sweep, s]
-        zsum_send[sweep] = total
-        copies = [
-            send(zsum_send.at[sweep], zsum_recv.at[sweep, s - 1], zs_send.at[sweep, s - 1],
-                 zs_recv.at[sweep, s - 1], dev_z(s))
-            for s in range(1, nz)
-        ]
-        for s, copy in enumerate(copies):
-            copy.wait_recv()
-            total = total + zsum_recv[sweep, s]
+            total = total + sum_recv[sweep, k]
         return total
 
     row_step = 128
@@ -482,9 +514,7 @@
             pltpu.VMEM((ny, nz, share, width), F32),
             pltpu.VMEM((share, width), F32),
             pltpu.VMEM((SWEEPS, 1, slots), F32),
-            pltpu.VMEM((SWEEPS, ny - 1, 1, slots), F32),
-            pltpu.VMEM((SWEEPS, 1, slots), F32),
-            pltpu.VMEM((SWEEPS, nz - 1, 1, slots), F32),
+            pltpu.VMEM((SWEEPS, ny * nz - 1, 1, slots), F32),
             *tile_shapes,
             dma,
             dma,
@@ -492,12 +522,13 @@
             dma((groups,)),
             dma((groups,)),
             dma((groups,)),
-            dma((SWEEPS, ny - 1)),
-            dma((SWEEPS, ny - 1)),
-            dma((SWEEPS, nz - 1)),
-            dma((SWEEPS, nz - 1)),
+            dma((groups,)),
+            dma((groups,)),
+            dma((SWEEPS, ny * nz - 1)),
+            dma((SWEEPS, ny * nz - 1)),
             dma((sems,)),
             dma((sems,)),
+            pltpu.SemaphoreType.REGULAR((3,)),
         ],
         compiler_params=pltpu.CompilerParams(
             collective_id=0, has_side_effects=True, vmem_limit_bytes=60 * 1024 * 1024
@@ -513,7 +544,7 @@
 
 
 def kernel_entry(ny, nz, nx, tiles, *refs):
-    head, rest = refs[:6 + 17], refs[6 + 17:]
+    head, rest = refs[:6 + 15], refs[6 + 15:]
     return kernel(ny, nz, nx, *head, rest[:tiles], *rest[tiles:])
 
 

time: 72.7 us -> 68.5 us (0.942)
  Pallas kernels: 70.8 us -> 66.6 us
    pallas_call x1, Pallas kernels: 70.8 us -> 66.6 us  [local(): pl.pallas_call(functools.partial(kernel_entry, ny, nz, nx, len(tile_shape...]
where the time goes in v4:
time: 68.5 us; the launch traced here: 68.2 us
  Pallas kernels  66.6 us (97%)
  local copies, waits for them, and re-layouts  1.54 us (2%)
    pallas_call x1, Pallas kernels, local(): pl.pallas_call(functools.partial(kernel_entry, ny, nz, nx, len(tile_shape...  66.6 us
    unnamed x1, local copies, waits for them, and re-layouts  1.54 us

profile of v4, /device:TPU:2, one launch (start us, length us, event | category | flops | bytes accessed | tf_op | source)
XLA Modules:
  0.0 68.2 jit_solution(3506361011598684902)
XLA Ops:
  0.0 66.6 %shard_map.55 = bf16[32,1536]{1,0:T(8,128)(2,1)} custom-call(bf16[256,1536]{1,0:T(8,128)(2,1)} %refs_0_.1, s32[1,2048]{1,0:T(1,128)} %bitcast.7, s32[1,128]{1,0:T(1,128)} %bitcast.8, s32[1,128]{1,0:T(1,128)} %bitcast.9, bf16[1024,1536]{1,0:T(8,128)(2,1)} %bitcast.5), custom_call_target="tpu_custom_call" | custom-call | tf_op jit(solution)/shard_map/pallas_call | solution.py:495
  66.6 1.5 %copy.7 = bf16[1,32,1536]{2,1,0:T(8,128)(2,1)} copy(bf16[1,32,1536]{2,1,0:T(8,128)(2,1)} %bitcast.6) | data formatting | bytes 196608

commit v5 on v4

--- a/solution.py
+++ b/solution.py
@@ -21,16 +21,16 @@
 
 GROUP = 256
 TILES = (
-    ("yz", 0, 256, -1, "direct"),
-    ("zy", 1, 128, 1, "direct"),
-    ("zy", 1, 128, -1, "direct"),
-    ("zy", 2, 128, -1, "direct"),
-    ("zy", 2, 128, 1, "direct"),
-    ("yz", 3, 256, 1, "direct"),
-    ("yz", 4, 128, -1, "ring"),
-    ("yz", 4, 128, 1, "ring"),
-    ("zy", 5, 128, -1, "direct"),
-    ("zy", 5, 128, 1, "direct"),
+    ("yz", 0, 256, -1, "direct", 0),
+    ("zy", 1, 128, 1, "direct", 0),
+    ("zy", 1, 128, -1, "direct", 0),
+    ("zy", 2, 128, -1, "direct", 0),
+    ("zy", 2, 128, 1, "direct", 0),
+    ("yz", 3, 256, 1, "direct", 0),
+    ("yz", 4, 128, -1, "ring", 0),
+    ("yz", 4, 128, 1, "ring", 0),
+    ("zy", 5, 128, -1, "direct", 0),
+    ("zy", 5, 128, 1, "direct", 0),
 )
 
 
@@ -44,16 +44,16 @@
 
 
 def tile_tasks(index, tile, sizes, slots):
-    order, group, cols, long, mode = tile
+    order, group, cols, long, mode, _ = tile
     share = slots
     for axis in order:
         share //= sizes[axis]
     before = ("product", group)
-    tasks = {before: ((), (), 0.68, ())}
+    tasks = {before: ((), (), 0.69, ())}
     for stage, axis in enumerate(order):
         n = sizes[axis]
         chunk = (slots // n if stage == 0 else share) * cols
-        work = chunk * 2.1e-6
+        work = chunk * 1.526e-6
         kind = "ring" if stage == 0 else mode
         messages = stage_messages(kind, n, long)
         names = [(index, stage, name, step) for name, step, _, _ in messages]
@@ -63,18 +63,18 @@
             for key, one in zip(names, wire):
                 last = key[:3] + (key[3] - 1,)
                 first = key[3] == 1
-                tasks[key] = ((before,) if first else (last,), () if first else (last,), work, (one,))
+                tasks[key] = ((before,) if first else (last,), () if first else (last,), work + 0.03, (one,))
             ends = [(index, stage, "far", n // 2)] + ([(index, stage, "near", n // 2 - 1)] if n > 2 else [])
-            tasks[done] = (tuple(ends), tuple(ends), 2 * work, ())
+            tasks[done] = (tuple(ends), tuple(ends), 2 * work + 0.03, ())
         else:
-            tasks[index, stage, "all"] = ((before,), (), n * work, tuple(wire))
-            tasks[done] = (((index, stage, "all"),), tuple(names), n * work, ())
+            tasks[index, stage, "all"] = ((before,), (), n * work + 0.03, tuple(wire))
+            tasks[done] = (((index, stage, "all"),), tuple(names), n * work + 0.03, ())
         before = done
     return tasks
 
 
 def schedule(sizes, slots):
-    rate, hop_us, next_hop_us = 46500.0, 2.2, 0.75
+    rate, hop_us, next_hop_us = 46500.0, 1.5, 0.75
     tasks = {}
     for index, tile in enumerate(TILES):
         tasks.update(tile_tasks(index, tile, sizes, slots))
@@ -92,6 +92,10 @@
             chain[key] = tasks[key][2] + max([gap + length(one) for one, gap in after[key]], default=0.0)
         return chain[key]
 
+    def rank(key):
+        heads = [one[0] for one, _ in after[key]] if key[0] == "product" else [key[0]]
+        return length(key) + max(TILES[index][5] for index in heads)
+
     now, order, arrival, link_free, done = 0.0, [], {}, {}, set()
     while len(order) < len(tasks):
         ready = []
@@ -100,9 +104,9 @@
                 ready.append((max([arrival[one] for one in waits], default=0.0), key))
         started = [one for one in ready if one[0] <= now]
         if started:
-            at, key = max(started, key=lambda one: length(one[1]))
+            at, key = max(started, key=lambda one: rank(one[1]))
         else:
-            at, key = min(ready, key=lambda one: (one[0], -length(one[1])))
+            at, key = min(ready, key=lambda one: (one[0], -rank(one[1])))
         now = max(now, at) + tasks[key][2]
         for name, axis, way, hops, size in tasks[key][3]:
             start = max(now, link_free.get((axis, way), 0.0))
@@ -124,10 +128,10 @@
 
 def kernel(
     ny, nz, nx,
-    points_hbm, parent_ref, owner_ref, count_ref, cent_hbm, out_ref,
-    point_raw, cent_raw, cent_unit, point_unit, packed, rows, member, onehot, place, weights, assign_t, part, final,
+    points_hbm, parent_hbm, owner_hbm, count_hbm, cent_hbm, out_ref,
+    parent_ref, owner_ref, count_ref, point_raw, cent_raw, cent_unit, point_unit, packed, rows, member, onehot, place, weights, assign_t, part, final,
     sum_send, sum_recv, tile_bufs,
-    point_sem, cent_sem, x_send, x_recv, l_send, l_recv, f_send, f_recv, s_send, s_recv, rs_send, rs_recv,
+    small_sem, point_sem, cent_sem, x_send, x_recv, l_send, l_recv, f_send, f_recv, s_send, s_recv, rs_send, rs_recv,
     round_sem,
 ):
     pts, me = lax.axis_index("pts"), lax.axis_index("own")
@@ -135,7 +139,7 @@
     x, core = lax.div(me, CORES), lax.rem(me, CORES)
     groups = nx * CORES
     tokens, width = points_hbm.shape
-    parents = owner_ref.shape[1]
+    parents = owner_hbm.shape[1]
     slots = cent_hbm.shape[0]
 
     def own_at(dx, dc, sign):
@@ -160,6 +164,14 @@
     peers += [dev_y(s) for s in range(1, ny)] + [dev_z(1), dev_z(-1)]
     for peer in peers:
         pl.semaphore_signal(barrier, inc=1, device_id=peer, device_id_type=MESH)
+    small = [
+        pltpu.make_async_copy(source, target, small_sem.at[i])
+        for i, (source, target) in enumerate(
+            ((owner_hbm, owner_ref), (count_hbm, count_ref), (parent_hbm, parent_ref))
+        )
+    ]
+    for copy in small:
+        copy.start()
     point_copy = pltpu.make_async_copy(points_hbm, point_raw, point_sem)
     point_copy.start()
     cent_copy = pltpu.make_async_copy(cent_hbm, cent_raw, cent_sem)
@@ -175,6 +187,9 @@
         copy.start()
         pending.append(copy)
         return copy
+
+    for copy in small:
+        copy.wait()
 
     square = (parents, parents)
     owner_row = owner_ref[...].astype(F32)
@@ -392,7 +407,7 @@
             part[:, :, :, span] = value.reshape(ny, nz, share, GROUP)
 
         steps["product", group] = product
-    for index, (order, group_of, cols, long, mode) in enumerate(TILES):
+    for index, (order, group_of, cols, long, mode, _) in enumerate(TILES):
         send1, recv1, middle, send2, recv2 = tile_bufs[5 * index:5 * index + 5]
         first = taken_columns[group_of]
         taken_columns[group_of] += cols
@@ -481,7 +496,7 @@
     groups = mesh_own
     tile_shapes = []
     sems = 0
-    for order, _, cols, _, _ in TILES:
+    for order, _, cols, _, _, _ in TILES:
         n1, n2 = (ny, nz) if order == "yz" else (nz, ny)
         tile_shapes += [
             pltpu.VMEM((n1 - 1, n2, share, cols), BF16),
@@ -492,14 +507,22 @@
         ]
         sems += n1 + n2 - 2
     dma = pltpu.SemaphoreType.DMA
+    operands = (
+        points,
+        parent_of.reshape(1, groups * tokens),
+        owner_of.reshape(1, parents),
+        child_count.reshape(1, parents),
+        centroids[0],
+    )
     out = pl.pallas_call(
         functools.partial(kernel_entry, ny, nz, nx, len(tile_shapes)),
         out_shape=jax.ShapeDtypeStruct((share, width), BF16),
-        in_specs=[pl.BlockSpec(memory_space=pl.ANY)]
-        + [pl.BlockSpec(memory_space=pltpu.VMEM)] * 3
-        + [pl.BlockSpec(memory_space=pl.ANY)],
+        in_specs=[pl.BlockSpec(memory_space=pl.ANY)] * 5,
         out_specs=pl.BlockSpec(memory_space=pltpu.VMEM),
         scratch_shapes=[
+            pltpu.VMEM((1, groups * tokens), jnp.int32),
+            pltpu.VMEM((1, parents), jnp.int32),
+            pltpu.VMEM((1, parents), jnp.int32),
             pltpu.VMEM((tokens, width), BF16),
             pltpu.VMEM((slots, width), BF16),
             pltpu.VMEM((slots, width), BF16),
@@ -516,6 +539,7 @@
             pltpu.VMEM((SWEEPS, 1, slots), F32),
             pltpu.VMEM((SWEEPS, ny * nz - 1, 1, slots), F32),
             *tile_shapes,
+            dma((3,)),
             dma,
             dma,
             dma((groups,)),
@@ -531,20 +555,16 @@
             pltpu.SemaphoreType.REGULAR((3,)),
         ],
         compiler_params=pltpu.CompilerParams(
-            collective_id=0, has_side_effects=True, vmem_limit_bytes=60 * 1024 * 1024
+            collective_id=0, has_side_effects=True, vmem_limit_bytes=36 * 1024 * 1024
         ),
     )(
-        points,
-        parent_of.reshape(1, groups * tokens),
-        owner_of.reshape(1, parents),
-        child_count.reshape(1, parents),
-        centroids[0],
+        *(pltpu.with_memory_space_constraint(one, pltpu.HBM) for one in operands)
     )
     return out[None]
 
 
 def kernel_entry(ny, nz, nx, tiles, *refs):
-    head, rest = refs[:6 + 15], refs[6 + 15:]
+    head, rest = refs[:6 + 18], refs[6 + 18:]
     return kernel(ny, nz, nx, *head, rest[:tiles], *rest[tiles:])
 
 

time: 68.5 us -> 66.2 us (0.966)
  Pallas kernels: 66.6 us -> 65.5 us
  local copies, waits for them, and re-layouts: 1.54 us -> 0.64 us
    pallas_call x1, Pallas kernels: 66.6 us -> 65.5 us  [local(): pl.pallas_call(functools.partial(kernel_entry, ny, nz, nx, len(tile_shape...]
    unnamed x1, local copies, waits for them, and re-layouts: 1.54 us -> 0.64 us
where the time goes in v5:
time: 66.2 us
  Pallas kernels  65.5 us (99%)
    pallas_call x1, Pallas kernels, local(): pl.pallas_call(functools.partial(kernel_entry, ny, nz, nx, len(tile_shape...  65.5 us

profile of v5, /device:TPU:2, one launch (start us, length us, event | category | flops | bytes accessed | tf_op | source)
XLA Modules:
  0.0 66.2 jit_solution(6886565790348692598)
XLA Ops:
  0.0 65.5 %shard_map.55 = bf16[32,1536]{1,0:T(8,128)(2,1)S(1)} custom-call(bf16[256,1536]{1,0:T(8,128)(2,1)} %refs_0_.1, s32[1,2048]{1,0:T(1,128)} %bitcast.7, s32[1,128]{1,0:T(1,128)} %bitcast.8, s32[1,128]{1,0:T(1,128)} %bitcast.9, bf16[1024,1536]{1,0:T(8,128)(2,1)} %bitcast.6), custom_call_target="tpu_custom_call" | custom-call | tf_op jit(solution)/shard_map/pallas_call | solution.py:517
  65.5 0.6 copy.7

commit v6 on v5

--- a/solution.py
+++ b/solution.py
@@ -13,6 +13,7 @@
 HALF = PAIR // 2
 EXTRA = CAP - HALF
 LAST = 384
+NEVER = -1e30
 CORES = 2
 NY = 4
 MESH = pl.DeviceIdType.MESH
@@ -332,31 +333,38 @@
             rows[span, depth], cent_unit[cols, depth], (((1,), (1,)), ((), ())), preferred_element_type=F32
         )
 
+    def allowed(span, cols):
+        return jnp.dot(onehot[span, :], member[:, cols], preferred_element_type=F32) > 0.5
+
     def weigh(span, cols, value):
-        allowed = jnp.dot(onehot[span, :], member[:, cols], preferred_element_type=F32)
-        value = jnp.where(allowed > 0.5, jnp.exp(value * scale), 0.0)
         weights[span, cols] = value
         return jnp.sum(value, axis=0, keepdims=True)
 
     first_rows = (1 + len(far)) * CORES * CAP
     top, bottom = slice(0, first_rows), slice(first_rows, groups * CAP)
     slot_cols = [slice(n * wide, (n + 1) * wide) for n in range(slots // wide)]
+    for cols in slot_cols:
+        weights[bottom, cols] = jnp.where(allowed(bottom, cols), 0.0, NEVER)
     arrivals[0, 1].wait_recv()
     hand_over(far, slice(0, width))
     handed_over(far)
-    sums = [weigh(top, cols, score(top, cols, slice(0, width))) for cols in slot_cols]
+    sums = [
+        weigh(top, cols, jnp.where(allowed(top, cols), jnp.exp(score(top, cols, slice(0, width)) * scale), 0.0))
+        for cols in slot_cols
+    ]
     pl.semaphore_wait(round_sem.at[1], 2)
     for step in (1, -1):
         pl.semaphore_signal(round_sem.at[2], inc=1, device_id=dev_z(step), device_id_type=MESH)
     hand_over(near, early)
     handed_over(near)
     for cols in slot_cols:
-        weights[bottom, cols] = score(bottom, cols, early)
+        weights[bottom, cols] += score(bottom, cols, early)
     for dx in near:
         for dc in range(CORES):
             lasts[dx, dc].wait_recv()
     for n, cols in enumerate(slot_cols):
-        sums[n] = sums[n] + weigh(bottom, cols, weights[bottom, cols] + score(bottom, cols, late))
+        value = jnp.exp((weights[bottom, cols] + score(bottom, cols, late)) * scale)
+        sums[n] = sums[n] + weigh(bottom, cols, value)
     column = jnp.concatenate(sums, axis=1)
     pl.semaphore_wait(round_sem.at[2], 2)
 
@@ -393,7 +401,7 @@
                 partial = jnp.sum(value, axis=0, keepdims=True)
                 column = partial if column is None else column + partial
             else:
-                assign_t[:, span] = jnp.transpose(value).astype(BF16)
+                assign_t[:, span] = jnp.transpose(value.astype(BF16))
 
     share = slots // (ny * nz)
     sizes = {"y": ny, "z": nz}
@@ -478,6 +486,8 @@
 
     for key in schedule(sizes, slots):
         steps[key]()
+        while len(pending) > 64:
+            pending.pop(0).wait_send()
 
     base = cent_unit[pl.ds(pl.multiple_of(pts * share, share), share), :].astype(F32)
     out_ref[...] = unit_rms(base + 8.0 * final[...]).astype(BF16)

time: 66.2 us -> 65.9 us (level)
  no operation moved by 1% of the time
where the time goes in v6:
time: 65.9 us; the launch traced here: 65.8 us
  Pallas kernels  65.2 us (99%)
    pallas_call x1, Pallas kernels, local(): pl.pallas_call(functools.partial(kernel_entry, ny, nz, nx, len(tile_shape...  65.2 us

profile of v6, /device:TPU:2, one launch (start us, length us, event | category | flops | bytes accessed | tf_op | source)
XLA Modules:
  0.0 65.8 jit_solution(13723388257870642057)
XLA Ops:
  0.0 65.2 %shard_map.55 = bf16[32,1536]{1,0:T(8,128)(2,1)S(1)} custom-call(bf16[256,1536]{1,0:T(8,128)(2,1)} %refs_0_.1, s32[1,2048]{1,0:T(1,128)} %bitcast.7, s32[1,128]{1,0:T(1,128)} %bitcast.8, s32[1,128]{1,0:T(1,128)} %bitcast.9, bf16[1024,1536]{1,0:T(8,128)(2,1)} %bitcast.6), custom_call_target="tpu_custom_call" | custom-call | tf_op jit(solution)/shard_map/pallas_call | solution.py:527
  65.2 0.6 copy.7

commit v7 on v6

--- a/solution.py
+++ b/solution.py
@@ -12,7 +12,7 @@
 PAIR = 96
 HALF = PAIR // 2
 EXTRA = CAP - HALF
-LAST = 384
+LAST = 512
 NEVER = -1e30
 CORES = 2
 NY = 4

time: 65.9 us -> 67.3 us (1.021)
  Pallas kernels: 65.2 us -> 66.6 us
    pallas_call x1, Pallas kernels: 65.2 us -> 66.6 us  [local(): pl.pallas_call(functools.partial(kernel_entry, ny, nz, nx, len(tile_shape...]
where the time goes in v7:
time: 67.3 us; the launch traced here: 67.2 us
  Pallas kernels  66.6 us (99%)
    pallas_call x1, Pallas kernels, local(): pl.pallas_call(functools.partial(kernel_entry, ny, nz, nx, len(tile_shape...  66.6 us

profile of v7, /device:TPU:2, one launch (start us, length us, event | category | flops | bytes accessed | tf_op | source)
XLA Modules:
  0.0 67.2 jit_solution(3337644353894748793)
XLA Ops:
  0.0 66.6 %shard_map.55 = bf16[32,1536]{1,0:T(8,128)(2,1)S(1)} custom-call(bf16[256,1536]{1,0:T(8,128)(2,1)} %refs_0_.1, s32[1,2048]{1,0:T(1,128)} %bitcast.7, s32[1,128]{1,0:T(1,128)} %bitcast.8, s32[1,128]{1,0:T(1,128)} %bitcast.9, bf16[1024,1536]{1,0:T(8,128)(2,1)} %bitcast.6), custom_call_target="tpu_custom_call" | custom-call | tf_op jit(solution)/shard_map/pallas_call | solution.py:527
  66.6 0.6 copy.7
